TPU v7x, 32 devices: a whole 2x2x4 slice. The times are simulated.
32 devices in a mesh: dp: 8 (over y, x, core), tensor: 4 (over z).
Axes of the slice: x: 2, y: 2, z: 4, core: 2. Of those that a mesh axis runs over, the one named last changes fastest.
Arguments:
- inputs: bfloat16 [32768, 768], P('dp'), may hold values from -6 to 6
- segments: int32 [64, 512], P('dp'), may hold values from 0 to 7, never falling along the last dimension, each value on 1 to 128 neighbouring positions
- w_query: bfloat16 [768, 768], P(None, 'tensor'), may hold values from -0.21875 to 0.21875
- w_key: bfloat16 [768, 768], P(None, 'tensor'), may hold values from -0.21875 to 0.21875
- w_value: bfloat16 [768, 768], P(None, 'tensor'), may hold values from -0.21875 to 0.21875
- b_query: bfloat16 [768], P('tensor'), may hold values from -3 to 3
- b_value: bfloat16 [768], P('tensor'), may hold values from -3 to 3
- w_output: bfloat16 [768, 768], P('tensor'), may hold values from -0.875 to 0.875
- b_output: bfloat16 [768], replicated, may hold values from -3 to 3
- gain_attn: bfloat16 [768], replicated, may hold values from 0.5 to 1.5
- shift_attn: bfloat16 [768], replicated, may hold values from -3 to 3
- w_hidden: bfloat16 [768, 3072], P(None, 'tensor'), may hold values from -0.21875 to 0.21875
- b_hidden: bfloat16 [3072], P('tensor'), may hold values from -3 to 3
- w_project: bfloat16 [3072, 768], P('tensor'), may hold values from -0.109375 to 0.109375
- b_project: bfloat16 [768], replicated, may hold values from -3 to 3
- gain_ffn: bfloat16 [768], replicated, may hold values from 0.5 to 1.5
- shift_ffn: bfloat16 [768], replicated, may hold values from -3 to 3
- cotangent: bfloat16 [32768, 768], P(('dp', 'tensor')), may hold values from -6 to 6
Outputs:
- output: bfloat16 [32768, 768], P(('dp', 'tensor'))
- grad_input: float32 [32768, 768], P(('dp', 'tensor'))
- grad_w_query: float32 [768, 768], P('dp', 'tensor')
- grad_w_key: float32 [768, 768], P('dp', 'tensor')
- grad_w_value: float32 [768, 768], P('dp', 'tensor')
- grad_w_output: float32 [768, 768], P('tensor', 'dp')
- grad_w_hidden: float32 [768, 3072], P('dp', 'tensor')
- grad_w_project: float32 [3072, 768], P('tensor', 'dp')
- grad_bias_qv: float32 [2, 12, 64], P(None, 'tensor', 'dp')
- grad_b_hidden: float32 [48, 64], P('tensor', 'dp')
- grad_vectors: float32 [6, 768], P(None, ('dp', 'tensor'))
Inputs may be any that keep to these rules, and one draw needn't show every extreme that they name: `segments`: within each row of 512 tokens segment numbers never fall; each text holds 1 to 128 tokens, and some text holds exactly 128.
All inputs are finite; a program needn't handle non-finite values.
Results may differ from a plain program's by a relative error of at most 0.014.
Values may be sent and summed in bfloat16 or wider, within the bound.
A program may use at most 192 MiB of HBM per device.

v0:
```python
import jax
import jax.numpy as jnp
from jax import lax
from jax.sharding import PartitionSpec as P

HD = 64
norm_epsilon = 1e-12
root_half = 0.7071067811865476


def norm_forward(values, norm_gain, norm_shift):
    average = jnp.mean(values, axis=-1, keepdims=True)
    centered = values - average
    variance = jnp.mean(centered * centered, axis=-1, keepdims=True)
    inverse = lax.rsqrt(variance + norm_epsilon)
    scaled = centered * inverse
    return (scaled * norm_gain + norm_shift, scaled, inverse)


def norm_backward(grad_out, scaled, inverse, norm_gain):
    weighted = grad_out * norm_gain
    mean_grad = jnp.mean(weighted, axis=-1, keepdims=True)
    mean_proj = jnp.mean(weighted * scaled, axis=-1, keepdims=True)
    return inverse * (weighted - mean_grad - scaled * mean_proj)


def gelu_exact(values):
    return 0.5 * values * (1.0 + lax.erf(values * root_half))


def cross_rows(left, right):
    return lax.dot_general(
        left, right, (((0,), (0,)), ((), ())), preferred_element_type=jnp.float32
    )


def times_transposed(left, right):
    return lax.dot_general(
        left, right, (((1,), (1,)), ((), ())), preferred_element_type=jnp.float32
    )


def masked_scores(queries, keys_in, segment_row):
    same_text = segment_row[:, None] == segment_row[None, :]
    scores = jnp.einsum("qhd,khd->hqk", queries, keys_in, preferred_element_type=jnp.float32)
    scores = scores * queries.shape[2] ** (-0.5)
    return jnp.where(same_text[None], scores, -1000000000.0)


def attend_forward(packed):
    queries, keys_in, values, segment_row = packed
    scores = masked_scores(queries, keys_in, segment_row)
    row_max = jnp.max(scores, axis=-1, keepdims=True)
    exponent = jnp.exp(scores - row_max)
    row_total = jnp.sum(exponent, axis=-1, keepdims=True)
    attn_probs = (exponent / row_total).astype(jnp.bfloat16)
    mixed_heads = jnp.einsum("hqk,khd->qhd", attn_probs, values, preferred_element_type=jnp.float32)
    return (mixed_heads.astype(jnp.bfloat16), row_max + jnp.log(row_total))


def attend_backward(packed):
    queries, keys_in, values, segment_row, logsum, grad_mixed = packed
    score_scale = queries.shape[2] ** (-0.5)
    scores = masked_scores(queries, keys_in, segment_row)
    attn_probs = jnp.exp(scores - logsum)
    grad_probs = jnp.einsum("qhd,khd->hqk", grad_mixed, values, preferred_element_type=jnp.float32)
    grad_values = jnp.einsum(
        "hqk,qhd->khd",
        attn_probs.astype(jnp.bfloat16),
        grad_mixed,
        preferred_element_type=jnp.float32,
    )
    inner_sum = jnp.sum(attn_probs * grad_probs, axis=-1, keepdims=True)
    grad_scores = (attn_probs * (grad_probs - inner_sum)).astype(jnp.bfloat16)
    grad_queries = (
        jnp.einsum("hqk,khd->qhd", grad_scores, keys_in, preferred_element_type=jnp.float32)
        * score_scale
    )
    grad_keys = (
        jnp.einsum("hqk,qhd->khd", grad_scores, queries, preferred_element_type=jnp.float32)
        * score_scale
    )
    return (
        grad_queries.astype(jnp.bfloat16),
        grad_keys.astype(jnp.bfloat16),
        grad_values.astype(jnp.bfloat16),
    )


def per_device(
    inputs,
    segments,
    w_query,
    w_key,
    w_value,
    b_query,
    b_value,
    w_output,
    b_output,
    gain_attn,
    shift_attn,
    w_hidden,
    b_hidden,
    w_project,
    b_project,
    gain_ffn,
    shift_ffn,
    cotangent,
):
    seq_len = segments.shape[1]
    row_count = segments.shape[0]
    token_count = inputs.shape[0]
    share_rows = cotangent.shape[0]
    offset = lax.axis_index("tensor") * share_rows
    head_width = w_query.shape[1]
    head_shape = (row_count, seq_len, head_width // HD, HD)
    attn_gain = gain_attn.astype(jnp.float32)
    attn_shift = shift_attn.astype(jnp.float32)
    attn_bias = b_output.astype(jnp.float32)
    ffn_gain = gain_ffn.astype(jnp.float32)
    ffn_shift = shift_ffn.astype(jnp.float32)
    ffn_bias = b_project.astype(jnp.float32)
    grad_out = cotangent.astype(jnp.float32)
    queries = (
        jnp.dot(inputs, w_query, preferred_element_type=jnp.float32) + b_query.astype(jnp.float32)
    ).astype(jnp.bfloat16)
    keys_in = jnp.dot(inputs, w_key, preferred_element_type=jnp.float32).astype(jnp.bfloat16)
    values = (
        jnp.dot(inputs, w_value, preferred_element_type=jnp.float32) + b_value.astype(jnp.float32)
    ).astype(jnp.bfloat16)
    query_heads = queries.reshape(head_shape)
    key_heads = keys_in.reshape(head_shape)
    value_heads = values.reshape(head_shape)
    mixed_heads, logsum = lax.map(attend_forward, (query_heads, key_heads, value_heads, segments))
    mixed_flat = mixed_heads.reshape(token_count, head_width)
    picked = mixed_flat
    branch_share = lax.psum_scatter(
        jnp.dot(picked, w_output, preferred_element_type=jnp.float32),
        "tensor",
        scatter_dimension=0,
        tiled=True,
    )
    input_share = lax.dynamic_slice_in_dim(inputs, offset, share_rows, 0).astype(jnp.float32)
    hidden_share = input_share + (branch_share + attn_bias)
    hidden_all = lax.all_gather(hidden_share, "tensor", axis=0, tiled=True)
    normed_all, scaled_all, inverse_all = norm_forward(hidden_all, attn_gain, attn_shift)
    normed_low = normed_all.astype(jnp.bfloat16)
    normed_share = lax.dynamic_slice_in_dim(normed_all, offset, share_rows, 0)
    scaled_share = lax.dynamic_slice_in_dim(scaled_all, offset, share_rows, 0)
    hidden_pre = jnp.dot(
        normed_low, w_hidden, preferred_element_type=jnp.float32
    ) + b_hidden.astype(jnp.float32)
    active, gelu_pull = jax.vjp(gelu_exact, hidden_pre)
    active_low = active.astype(jnp.bfloat16)
    picked = active_low
    second_share = lax.psum_scatter(
        jnp.dot(picked, w_project, preferred_element_type=jnp.float32),
        "tensor",
        scatter_dimension=0,
        tiled=True,
    )
    block_sum = normed_share + (second_share + ffn_bias)
    output_share, scaled_out, inverse_out = norm_forward(block_sum, ffn_gain, ffn_shift)
    grad_sum = norm_backward(grad_out, scaled_out, inverse_out, ffn_gain)
    grad_ffn_gain = jnp.sum(grad_out * scaled_out, axis=0)
    grad_ffn_shift = jnp.sum(grad_out, axis=0)
    grad_sum_low = grad_sum.astype(jnp.bfloat16)
    grad_ffn_bias = jnp.sum(grad_sum_low.astype(jnp.float32), axis=0)
    grad_sum_all = lax.all_gather(grad_sum_low, "tensor", axis=0, tiled=True)
    grad_active = times_transposed(grad_sum_all, w_project)
    grad_w_project = cross_rows(active_low, grad_sum_all)
    grad_hidden_pre = gelu_pull(grad_active)[0].astype(jnp.bfloat16)
    grad_b_hidden = jnp.sum(grad_hidden_pre.astype(jnp.float32), axis=0).reshape(-1, HD)
    grad_w_hidden = cross_rows(normed_low, grad_hidden_pre)
    picked = grad_hidden_pre
    grad_normed_share = grad_sum + lax.psum_scatter(
        times_transposed(picked, w_hidden), "tensor", scatter_dimension=0, tiled=True
    )
    grad_normed_all = lax.all_gather(grad_normed_share, "tensor", axis=0, tiled=True)
    grad_hidden_all = norm_backward(grad_normed_all, scaled_all, inverse_all, attn_gain)
    grad_hidden_share = lax.dynamic_slice_in_dim(grad_hidden_all, offset, share_rows, 0)
    grad_hidden_low = grad_hidden_all.astype(jnp.bfloat16)
    grad_attn_gain = jnp.sum(grad_normed_share * scaled_share, axis=0)
    grad_attn_shift = jnp.sum(grad_normed_share, axis=0)
    grad_attn_bias = jnp.sum(grad_hidden_share.astype(jnp.bfloat16).astype(jnp.float32), axis=0)
    grad_w_output = cross_rows(mixed_flat, grad_hidden_low)
    grad_mixed = (
        times_transposed(grad_hidden_low, w_output).astype(jnp.bfloat16).reshape(head_shape)
    )
    grad_query_heads, grad_key_heads, grad_value_heads = lax.map(
        attend_backward, (query_heads, key_heads, value_heads, segments, logsum, grad_mixed)
    )
    grad_queries = grad_query_heads.reshape(token_count, head_width)
    grad_keys = grad_key_heads.reshape(token_count, head_width)
    grad_values = grad_value_heads.reshape(token_count, head_width)
    grad_w_query = cross_rows(inputs, grad_queries)
    grad_w_key = cross_rows(inputs, grad_keys)
    grad_w_value = cross_rows(inputs, grad_values)
    grad_b_query = jnp.sum(grad_queries.astype(jnp.float32), axis=0)
    grad_b_value = jnp.sum(grad_values.astype(jnp.float32), axis=0)
    grad_bias_qv = jnp.stack([grad_b_query, grad_b_value]).reshape(2, head_width // HD, HD)
    summed = times_transposed(grad_queries, w_query)
    summed = summed + times_transposed(grad_keys, w_key)
    grad_input = grad_hidden_share + lax.psum_scatter(
        (summed + times_transposed(grad_values, w_value)).astype(jnp.bfloat16),
        "tensor",
        scatter_dimension=0,
        tiled=True,
    ).astype(jnp.float32)
    all_parts = (
        lax.psum_scatter(grad_w_query, "dp", scatter_dimension=0, tiled=True),
        lax.psum_scatter(grad_w_key, "dp", scatter_dimension=0, tiled=True),
        lax.psum_scatter(grad_w_value, "dp", scatter_dimension=0, tiled=True),
        lax.psum_scatter(grad_w_output, "dp", scatter_dimension=1, tiled=True),
        lax.psum_scatter(grad_w_hidden, "dp", scatter_dimension=0, tiled=True),
        lax.psum_scatter(grad_w_project, "dp", scatter_dimension=1, tiled=True),
        lax.psum_scatter(grad_bias_qv, "dp", scatter_dimension=2, tiled=True),
        lax.psum_scatter(grad_b_hidden, "dp", scatter_dimension=1, tiled=True),
    )
    (
        sum_query,
        sum_key,
        sum_value,
        sum_output,
        sum_hidden,
        sum_project,
        sum_bias_qv,
        sum_b_hidden,
    ) = all_parts
    vector_stack = jnp.stack(
        [
            grad_attn_gain,
            grad_attn_shift,
            grad_attn_bias,
            grad_ffn_gain,
            grad_ffn_shift,
            grad_ffn_bias,
        ]
    )
    sum_vectors = lax.psum_scatter(vector_stack, ("dp", "tensor"), scatter_dimension=1, tiled=True)
    return (
        output_share.astype(jnp.bfloat16),
        grad_input,
        sum_query,
        sum_key,
        sum_value,
        sum_output,
        sum_hidden,
        sum_project,
        sum_bias_qv,
        sum_b_hidden,
        sum_vectors,
    )


def solution(mesh):
    in_specs = (
        P("dp", None),
        P("dp", None),
        P(None, "tensor"),
        P(None, "tensor"),
        P(None, "tensor"),
        P("tensor"),
        P("tensor"),
        P("tensor", None),
        P(),
        P(),
        P(),
        P(None, "tensor"),
        P("tensor"),
        P("tensor", None),
        P(),
        P(),
        P(),
        P(("dp", "tensor"), None),
    )
    out_specs = (
        P(("dp", "tensor"), None),
        P(("dp", "tensor"), None),
        P("dp", "tensor"),
        P("dp", "tensor"),
        P("dp", "tensor"),
        P("tensor", "dp"),
        P("dp", "tensor"),
        P("tensor", "dp"),
        P(None, "tensor", "dp"),
        P("tensor", "dp"),
        P(None, ("dp", "tensor")),
    )
    return jax.shard_map(
        per_device, mesh=mesh, in_specs=in_specs, out_specs=out_specs, check_vma=False
    )
```

profile of v0, /device:TPU:0, one launch (start us, length us, event | category | flops | bytes accessed | tf_op | source)
XLA Modules:
  0.0 1853.3 jit_solution(15079120562952520668)
XLA Ops:
  8.7 5.0 fusion.54
  26.3 48.8 %while.26 = (s32[]{:T(128)}, bf16[8,512,3,64]{1,3,2,0:T(8,128)(2,1)}, f32[8,3,512,1]{2,1,3,0:T(4,128)S(1)}, bf16[8,512,3,64]{1,3,2,0:T(8,128)(2,1)}, s32[8,512]{...) while((s32[]{:T(128)}, ...), condition=%wide.region_3.4_spmd, body=%wide.region_0.3_spmd.sunk | while | flops 211122688 | bytes 11335781 | solution.py:134
  29.8 2.7 fusion.138
  35.9 2.7 fusion.138
  42.0 2.7 fusion.138
  48.0 2.7 fusion.138
  54.1 2.7 fusion.138
  60.2 2.7 fusion.138
  75.0 2.9 copy.70
  78.6 6.4 fusion.79
  85.7 214.1 %reduce-scatter.22.cloned.1.call-done = f32[1024,768]{1,0:T(8,128)} async-done(((f32[4096,768]{1,0:T(8,128)}), f32[1024,768]{1,0:T(8,128)}) %reduce-scatter.22.cloned.1.call-update) | async-done | bytes 3145744 | tf_op jit(solution)/shard_map/reduce_scatter | solution.py:137
  299.8 4.3 add_add_fusion.1
  304.9 218.7 %all-gather.4.cloned.1.call-done = f32[4096,768]{1,0:T(8,128)} async-done(((f32[1024,768]{1,0:T(8,128)}), f32[4096,768]{1,0:T(8,128)}) %all-gather.4.cloned.1.call-update) | async-done | bytes 12582928 | tf_op jit(solution)/shard_map/all_gather | solution.py:145
  523.6 5.2 reduce_sum.171
  528.8 6.0 multiply_reduce_fusion.2
  534.8 11.5 multiply_add_fusion
  546.3 10.4 multiply_convert_fusion.1
  556.8 10.6 fusion.80
  568.0 209.6 %reduce-scatter.24.cloned.1.call-done = f32[1024,768]{1,0:T(8,128)} async-done(((f32[4096,768]{1,0:T(8,128)}), f32[1024,768]{1,0:T(8,128)}) %reduce-scatter.24.cloned.1.call-update) | async-done | bytes 3145744 | tf_op jit(solution)/shard_map/reduce_scatter | solution.py:156
  777.6 3.3 fusion.78
  788.5 116.4 %all-gather.6.cloned.1.call-done = bf16[4096,768]{1,0:T(8,128)(2,1)} async-done(((bf16[1024,768]{1,0:T(8,128)(2,1)}), bf16[4096,768]{1,0:T(8,128)(2,1)}) %all-gather.6.cloned.1.call-update) | async-done | bytes 6291472 | tf_op jit(solution)/shard_map/all_gather | solution.py:169
  905.0 13.3 convert_reduce_fusion
  920.9 8.3 fusion.81
  929.9 209.5 %reduce-scatter.26.cloned.1.call-done = f32[1024,768]{1,0:T(8,128)} async-done(((f32[4096,768]{1,0:T(8,128)}), f32[1024,768]{1,0:T(8,128)}) %reduce-scatter.26.cloned.1.call-update) | async-done | bytes 3145744 | tf_op jit(solution)/shard_map/reduce_scatter | solution.py:176
  1139.4 6.4 fusion.75
  1145.9 219.3 %all-gather.8.cloned.1.call-done = f32[4096,768]{1,0:T(8,128)} async-done(((f32[1024,768]{1,0:T(8,128)}), f32[4096,768]{1,0:T(8,128)}) %all-gather.8.cloned.1.call-update) | async-done | bytes 12582928 | tf_op jit(solution)/shard_map/all_gather | solution.py:179
  1365.2 9.9 multiply_reduce_fusion.3
  1375.1 9.7 subtract_multiply_fusion
  1384.8 4.5 copy-done.2
  1389.2 3.5 fusion.70
  1392.7 6.8 convolution_convert_fusion
  1404.8 91.0 %while.27 = (s32[]{:T(128)}, bf16[8,512,3,64]{1,3,2,0:T(8,128)(2,1)}, bf16[8,512,3,64]{1,3,2,0:T(8,128)(2,1)}, bf16[8,512,3,64]{1,3,2,0:T(8,128)(2,1)S(1)}, bf16...) while((s32[]{:T(128)}, ...), condition=%wide.region_17.18_spmd, body=%wide.region_15.17_spmd.sunk | while | flops 511146496 | bytes 26125436 | solution.py:190
  1502.3 6.3 fusion.83
  1508.6 6.5 fusion.82
  1515.1 12.8 add_convert_fusion
  1527.9 11.9 fusion.66
  1539.8 10.1 fusion.84
  1550.0 4.7 convolution_bitcast_fusion.2
  1556.0 4.7 convolution_bitcast_fusion
  1563.4 4.7 convolution_bitcast_fusion.1
  1571.3 24.6 %all-reduce.3 = (f32[2,3,64]{2,1,0:T(4,128)S(1)}, f32[12,64]{1,0:T(8,128)S(1)}) all-reduce(f32[2,3,64]{2,1,0:T(4,128)S(1)} %pad_maximum_fusion, f32[12,64]{1,0:T(8,128)S(1)} %reshape.201), channel_id=12, replica_groups=mesh['dp'=8,'tensor'=4] {'dp'}, use_global_device_ids=true, to_apply=%region_27.28.clone | all-reduce | flops 1152 | bytes 9216
  1599.0 37.9 %reduce-scatter.28.cloned.1.call-done = bf16[1024,768]{1,0:T(8,128)(2,1)} async-done(((bf16[4096,768]{1,0:T(8,128)(2,1)}), bf16[1024,768]{1,0:T(8,128)(2,1)}) %reduce-scatter.28.cloned.1.call-update) | async-done | bytes 1572880 | tf_op jit(solution)/shard_map/reduce_scatter | solution.py:204
  1636.9 5.4 convert_reduce_fusion.3
  1642.4 41.1 %all-reduce.2 = f32[6,768]{1,0:T(8,128)S(1)} all-reduce(f32[6,768]{1,0:T(8,128)S(1)} %stack.39), channel_id=14, replica_groups=mesh['dp'=8,'tensor'=4] {'dp','tensor'}, use_global_device_ids=true, to_apply=%region_36.37.clone | all-reduce | flops 4608 | bytes 36864
  1684.4 46.0 %reduce-scatter.32.cloned.1.call-done = f32[768,96]{0,1:T(8,128)} async-done(((f32[768,768]{0,1:T(8,128)}), f32[768,96]{0,1:T(8,128)}) %reduce-scatter.32.cloned.1.call-update) | async-done | bytes 294928 | tf_op jit(solution)/shard_map/reduce_scatter | solution.py:216
  1730.4 38.7 %reduce-scatter.34.cloned.1.call-done = f32[96,192]{1,0:T(8,128)} async-done(((f32[768,192]{1,0:T(8,128)}), f32[96,192]{1,0:T(8,128)}) %reduce-scatter.34.cloned.1.call-update) | async-done | bytes 73744
  1769.1 38.5 %reduce-scatter.38.cloned.1.call-done = f32[96,192]{1,0:T(8,128)} async-done(((f32[768,192]{1,0:T(8,128)}), f32[96,192]{1,0:T(8,128)}) %reduce-scatter.38.cloned.1.call-update) | async-done | bytes 73744
  1807.6 38.7 %reduce-scatter.36.cloned.1.call-done = f32[96,192]{1,0:T(8,128)} async-done(((f32[768,192]{1,0:T(8,128)}), f32[96,192]{1,0:T(8,128)}) %reduce-scatter.36.cloned.1.call-update) | async-done | bytes 73744
  (267 shorter events, 172.8 us)
Async XLA Ops:
  7.2 539.1 %copy-start = (bf16[768,768]{1,0:T(8,128)(2,1)S(1)}, bf16[768,768]{1,0:T(8,128)(2,1)}, u32[]{:S(2)}) copy-start(bf16[768,768]{1,0:T(8,128)(2,1)} %param.33) | copy-start | bytes 3538948
  7.2 292.6 %reduce-scatter.22.cloned.1.call-start = ((), (), s32[]{:S(2)}) async-start(), calls=%async_computation.10 | async-start | bytes 15728640 | tf_op jit(solution)/shard_map/reduce_scatter | solution.py:137
  8.6 7.3 copy-start.17
  13.7 3.4 copy-start.13
  19.2 1.2 copy-start.15
  75.0 2.9 copy-start.8
  75.0 3.5 copy-start.12
  85.0 0.7 copy-start.23
  85.1 438.5 %all-gather.4.cloned.1.call-start = ((), (), s32[]{:S(2)}) async-start(), calls=%async_computation.11 | async-start | bytes 15728640 | tf_op jit(solution)/shard_map/all_gather | solution.py:145
  304.1 0.7 copy-start.24
  304.1 0.7 copy-start.25
  304.2 0.7 copy-start.26
  304.2 473.4 %reduce-scatter.24.cloned.1.call-start = ((), (), s32[]{:S(2)}) async-start(), calls=%async_computation.12 | async-start | bytes 15728640 | tf_op jit(solution)/shard_map/reduce_scatter | solution.py:156
  546.3 10.5 copy-start.3
  546.3 10.4 copy-start.30
  567.3 0.7 copy-start.27
  567.3 0.7 copy-start.28
  567.4 337.6 %all-gather.6.cloned.1.call-start = ((), (), s32[]{:S(2)}) async-start(), calls=%async_computation.13 | async-start | bytes 7864320 | tf_op jit(solution)/shard_map/all_gather | solution.py:169
  780.9 4.9 copy-start.4
  780.9 2.5 copy-start.6
  788.5 351.0 %reduce-scatter.26.cloned.1.call-start = ((), (), s32[]{:S(2)}) async-start(), calls=%async_computation.14 | async-start | bytes 15728640 | tf_op jit(solution)/shard_map/reduce_scatter | solution.py:176
  918.3 2.6 copy-start.5
  929.2 0.7 copy-start.29
  929.2 436.0 %all-gather.8.cloned.1.call-start = ((), (), s32[]{:S(2)}) async-start(), calls=%async_computation.15 | async-start | bytes 15728640 | tf_op jit(solution)/shard_map/all_gather | solution.py:179
  1145.8 451.5 %reduce-scatter.40.cloned.1.call-start = ((), (), s32[]{:S(2)}) async-start(), calls=%async_computation.22 | async-start | bytes 884736
  1384.8 4.5 copy-start.2
  1399.5 237.4 %reduce-scatter.28.cloned.1.call-start = ((), (), s32[]{:S(2)}) async-start(), calls=%async_computation.16 | async-start | bytes 7864320 | tf_op jit(solution)/shard_map/reduce_scatter | solution.py:204
  1498.7 3.5 copy-start.9
  1498.7 2.0 copy-start.7
  1500.3 14.8 copy-start.11
  1500.7 1.6 copy-start.16
  1502.2 6.4 copy-start.10
  1502.3 6.3 copy-start.18
  1508.6 6.5 copy-start.14
  1527.9 156.5 %reduce-scatter.30.cloned.1.call-start = ((), (), s32[]{:S(2)}) async-start(), calls=%async_computation.17 | async-start | bytes 2654208 | tf_op jit(solution)/shard_map/reduce_scatter | solution.py:215
  1539.8 190.6 %reduce-scatter.32.cloned.1.call-start = ((), (), s32[]{:S(2)}) async-start(), calls=%async_computation.18 | async-start | bytes 2654208 | tf_op jit(solution)/shard_map/reduce_scatter | solution.py:216
  1550.0 219.1 %reduce-scatter.34.cloned.1.call-start = ((), (), s32[]{:S(2)}) async-start(), calls=%async_computation.19 | async-start | bytes 884736
  1555.9 6.1 copy-start.31
  1555.9 7.3 copy-start.21
  1556.0 7.3 copy-start.20
  1556.0 7.3 copy-start.19
  1556.0 7.3 copy-start.22
  1556.0 251.6 %reduce-scatter.38.cloned.1.call-start = ((), (), s32[]{:S(2)}) async-start(), calls=%async_computation.21 | async-start | bytes 884736
  1561.9 284.3 %reduce-scatter.36.cloned.1.call-start = ((), (), s32[]{:S(2)}) async-start(), calls=%async_computation.20 | async-start | bytes 884736
  1597.3 249.0 %copy-start.1 = (bf16[768,768]{1,0:T(8,128)(2,1)S(1)}, bf16[768,768]{1,0:T(8,128)(2,1)}, u32[]{:S(2)}) copy-start(bf16[768,768]{1,0:T(8,128)(2,1)} %param.33) | copy-start | bytes 3538948
Sparse Core Ops, SparseCore 0:
  85.2 214.6 reduce-scatter.21
  304.3 219.2 all-gather.3
  567.5 210.0 reduce-scatter.23
  788.6 116.3 all-gather.5
  929.3 210.0 reduce-scatter.25
  1145.9 219.2 all-gather.7
  1399.7 33.1 reduce-scatter.39
  1528.0 108.9 reduce-scatter.27
  1640.9 43.4 reduce-scatter.29
  1688.2 42.1 reduce-scatter.31
  1734.1 34.9 reduce-scatter.33
  1772.6 34.9 reduce-scatter.37
  1811.3 34.9 reduce-scatter.35
where the time goes:
time: 1860 us; the launch traced here: 1850 us
  waiting for transfers between devices  1390 us (75%)
  matrix products  242 us (13%)
  other arithmetic  86.3 us (5%)
  blocking collectives  65.7 us (4%)
  local copies, waits for them, and re-layouts  54.6 us (3%)
    all_gather x1, waiting for transfers between devices, per_device(): lax.all_gather(grad_normed_share, 'tensor', axis=0, tiled=True)  219 us
    all_gather x1, waiting for transfers between devices, per_device(): hidden_all = lax.all_gather(hidden_share, 'tensor', axis=0, tiled=True)  219 us
    reduce_scatter x1, waiting for transfers between devices, per_device(): lax.psum_scatter(jnp.dot(picked, w_output, preferred_element_type=jnp.flo...  214 us
    reduce_scatter x1, waiting for transfers between devices, per_device(): lax.psum_scatter(jnp.dot(picked, w_project, preferred_element_type=jnp.fl...  210 us
    reduce_scatter x1, waiting for transfers between devices, per_device(): lax.psum_scatter(times_transposed(picked, w_hidden), 'tensor', scatter_di...  210 us
    all_gather x1, waiting for transfers between devices, per_device(): grad_sum_all = lax.all_gather(grad_sum_low, 'tensor', axis=0, tiled=True)  116 us
    unnamed x17, waiting for transfers between devices  116 us
    unnamed x2, blocking collectives  65.7 us
  transfers between devices with their start and end apart: 13, of which 12 were waited for; matrix products, arithmetic and copies ran while one was open for 10% of the time, Pallas kernels for 0%

commit v1 on v0

--- a/solution.py
+++ b/solution.py
@@ -2,10 +2,18 @@
 import jax.numpy as jnp
 from jax import lax
 from jax.sharding import PartitionSpec as P
+from jax.lax import axis_index, ppermute, psum
 
 HD = 64
 norm_epsilon = 1e-12
 root_half = 0.7071067811865476
+
+
+def hold_the_flows(inner_x, dim_no):
+    z1 = list(inner_x.shape[1:])
+    z1[dim_no] *= inner_x.shape[0]
+    after = jnp.moveaxis(inner_x, 0, dim_no).reshape(z1)
+    return after
 
 
 def norm_forward(values, norm_gain, norm_shift):
@@ -142,7 +150,24 @@
     )
     input_share = lax.dynamic_slice_in_dim(inputs, offset, share_rows, 0).astype(jnp.float32)
     hidden_share = input_share + (branch_share + attn_bias)
-    hidden_all = lax.all_gather(hidden_share, "tensor", axis=0, tiled=True)
+    full_n = psum(1, "tensor")
+    pile = []
+    for nth in range(full_n):
+        pile.append((nth, (nth + 1) % full_n))
+    slots = []
+    for to_i, j in pile:
+        slots.append((j, to_i))
+    raw_out, last = ([], [])
+    for dev in range(full_n - 1):
+        if dev % 2 == 0:
+            everything = ppermute(raw_out[-1] if raw_out else hidden_share, "tensor", perm=pile)
+            raw_out.append(everything)
+        else:
+            last.append(ppermute(last[-1] if last else hidden_share, "tensor", slots))
+    s_next = jnp.stack([*raw_out[::-1], hidden_share, *last])
+    y1 = axis_index("tensor") - len(raw_out)
+    s_next = s_next[(jnp.arange(full_n) - y1) % full_n]
+    hidden_all = hold_the_flows(s_next, 0)
     normed_all, scaled_all, inverse_all = norm_forward(hidden_all, attn_gain, attn_shift)
     normed_low = normed_all.astype(jnp.bfloat16)
     normed_share = lax.dynamic_slice_in_dim(normed_all, offset, share_rows, 0)

time: 1860 us -> 1890 us (1.016)
  waiting for transfers between devices: 1390 us -> 1310 us
  starting transfers between devices: 0.54 us -> 71.2 us
  local copies, waits for them, and re-layouts: 54.6 us -> 75.6 us
    all_gather x1 -> x0, waiting for transfers between devices: 219 us -> none  [per_device(): hidden_all = lax.all_gather(hidden_share, 'tensor', axis=0, tiled=True)]
    ppermute x0 -> x3, waiting for transfers between devices: none -> 136 us  [the longest x2 136 us: per_device(): ppermute(raw_out[-1] if raw_out else hidden_share, 'tensor', perm=pile)]
    ppermute x0 -> x3, starting transfers between devices: none -> 70.6 us  [the longest x2 68.2 us: per_device(): ppermute(raw_out[-1] if raw_out else hidden_share, 'tensor', perm=pile)]
    unnamed x17 -> x16, waiting for transfers between devices: 116 us -> 116 us
  transfers between devices with their start and end apart: 13 -> 15, of which waited for: 12 -> 14; matrix products, arithmetic and copies ran while one was open for 10% -> 10% of each run, Pallas kernels for 0% -> 0%
where the time goes in v1:
time: 1890 us; the launch traced here: 1880 us
  waiting for transfers between devices  1310 us (69%)
  matrix products  243 us (13%)
  other arithmetic  99.1 us (5%)
  local copies, waits for them, and re-layouts  75.6 us (4%)
  starting transfers between devices  71.2 us (4%)
  blocking collectives  65.5 us (3%)
    all_gather x1, waiting for transfers between devices, per_device(): lax.all_gather(grad_normed_share, 'tensor', axis=0, tiled=True)  219 us
    reduce_scatter x1, waiting for transfers between devices, per_device(): lax.psum_scatter(jnp.dot(picked, w_output, preferred_element_type=jnp.flo...  214 us
    reduce_scatter x1, waiting for transfers between devices, per_device(): lax.psum_scatter(jnp.dot(picked, w_project, preferred_element_type=jnp.fl...  211 us
    reduce_scatter x1, waiting for transfers between devices, per_device(): lax.psum_scatter(times_transposed(picked, w_hidden), 'tensor', scatter_di...  210 us
    ppermute x2, waiting for transfers between devices, per_device(): ppermute(raw_out[-1] if raw_out else hidden_share, 'tensor', perm=pile)  136 us
    all_gather x1, waiting for transfers between devices, per_device(): grad_sum_all = lax.all_gather(grad_sum_low, 'tensor', axis=0, tiled=True)  116 us
    unnamed x16, waiting for transfers between devices  116 us
    ppermute x2, starting transfers between devices, per_device(): ppermute(raw_out[-1] if raw_out else hidden_share, 'tensor', perm=pile)  68.2 us
  transfers between devices with their start and end apart: 15, of which 14 were waited for; matrix products, arithmetic and copies ran while one was open for 10% of the time, Pallas kernels for 0%

profile of v1, /device:TPU:0, one launch (start us, length us, event | category | flops | bytes accessed | tf_op | source)
XLA Modules:
  0.0 1877.6 jit_solution(16767544852023325276)
XLA Ops:
  8.7 5.0 fusion.55
  26.3 53.6 %while.26 = (s32[]{:T(128)}, bf16[8,512,3,64]{1,3,2,0:T(8,128)(2,1)}, f32[8,3,512,1]{2,1,3,0:T(4,128)}, bf16[8,512,3,64]{1,3,2,0:T(8,128)(2,1)}, s32[8,512]{1,0:...) while((s32[]{:T(128)}, bf16[8,512,3,64]{1,3,2,0:T(8,128)(2,1)}, ...), condition=%wide.region_3.4_spmd, body=%wide.region_0.3_spmd.sunk | while | flops 211122688 | bytes 11331685 | solution.py:142
  30.1 2.7 fusion.143
  36.7 2.7 fusion.143
  79.9 2.9 copy.70
  84.5 6.4 fusion.84
  91.7 214.1 %reduce-scatter.22.cloned.1.call-done = f32[1024,768]{1,0:T(8,128)} async-done(((f32[4096,768]{1,0:T(8,128)}), f32[1024,768]{1,0:T(8,128)}) %reduce-scatter.22.cloned.1.call-update) | async-done | bytes 3145744 | tf_op jit(solution)/shard_map/reduce_scatter | solution.py:145
  305.8 4.3 add_add_fusion.1
  313.9 69.3 %collective-permute-done = f32[1024,768]{1,0:T(8,128)} collective-permute-done((f32[1024,768]{1,0:T(8,128)}, f32[1024,768]{1,0:T(8,128)}, u32[]{:S(2)}, u32[]{:S(2)}) %collective-permute-start) | collective-permute-done | bytes 3145760 | tf_op jit(solution)/shard_map/ppermute | solution.py:163
  383.3 66.7 %collective-permute-start.1 = (f32[1024,768]{1,0:T(8,128)}, f32[1024,768]{1,0:T(8,128)}, u32[]{:S(2)}, u32[]{:S(2)}) collective-permute-start(f32[1024,768]{1,0:T(8,128)} %collective-permute-done), channel_id=1, source_target_pairs={{0,1},{1,2},{2,3},{3,0},{4,5},{5,6},{6,7},{7,4},{8,9},{9,10},{10,1... | collective-permute-start | bytes 9437192 | tf_op jit(solution)/shard_map/ppermute | solution.py:163
  450.6 66.3 %collective-permute-done.1 = f32[1024,768]{1,0:T(8,128)} collective-permute-done((f32[1024,768]{1,0:T(8,128)}, f32[1024,768]{1,0:T(8,128)}, u32[]{:S(2)}, u32[]{:S(2)}) %collective-permute-start.1) | collective-permute-done | bytes 3145760 | tf_op jit(solution)/shard_map/ppermute | solution.py:163
  516.9 10.5 pad_maximum_fusion
  527.4 10.4 gather_fusion
  537.8 5.2 reduce_sum.171
  543.0 6.2 multiply_reduce_fusion.2
  551.2 9.2 multiply_add_fusion
  560.4 13.8 multiply_convert_fusion.1
  576.8 8.1 fusion.85
  585.6 210.6 %reduce-scatter.24.cloned.1.call-done = f32[1024,768]{1,0:T(8,128)} async-done(((f32[4096,768]{1,0:T(8,128)}), f32[1024,768]{1,0:T(8,128)}) %reduce-scatter.24.cloned.1.call-update) | async-done | bytes 3145744 | tf_op jit(solution)/shard_map/reduce_scatter | solution.py:181
  796.2 3.3 fusion.82
  807.1 116.4 %all-gather.3.cloned.1.call-done = bf16[4096,768]{1,0:T(8,128)(2,1)} async-done(((bf16[1024,768]{1,0:T(8,128)(2,1)}), bf16[4096,768]{1,0:T(8,128)(2,1)}) %all-gather.3.cloned.1.call-update) | async-done | bytes 6291472 | tf_op jit(solution)/shard_map/all_gather | solution.py:194
  923.5 13.7 convert_reduce_fusion
  939.9 8.3 fusion.86
  948.8 209.6 %reduce-scatter.26.cloned.1.call-done = f32[1024,768]{1,0:T(8,128)} async-done(((f32[4096,768]{1,0:T(8,128)}), f32[1024,768]{1,0:T(8,128)}) %reduce-scatter.26.cloned.1.call-update) | async-done | bytes 3145744 | tf_op jit(solution)/shard_map/reduce_scatter | solution.py:201
  1158.4 6.0 fusion.79
  1164.5 219.3 %all-gather.5.cloned.1.call-done = f32[4096,768]{1,0:T(8,128)} async-done(((f32[1024,768]{1,0:T(8,128)}), f32[4096,768]{1,0:T(8,128)}) %all-gather.5.cloned.1.call-update) | async-done | bytes 12582928 | tf_op jit(solution)/shard_map/all_gather | solution.py:204
  1383.8 9.7 multiply_reduce_fusion.3
  1393.5 9.8 subtract_multiply_fusion
  1403.3 4.5 copy-done.2
  1407.8 3.5 fusion.71
  1411.3 6.8 convolution_convert_fusion
  1423.5 96.3 %while.27 = (s32[]{:T(128)}, bf16[8,512,3,64]{1,3,2,0:T(8,128)(2,1)}, bf16[8,512,3,64]{1,3,2,0:T(8,128)(2,1)}, bf16[8,512,3,64]{1,3,2,0:T(8,128)(2,1)S(1)}, bf16...) while((s32[]{:T(128)}, ...), condition=%wide.region_17.18_spmd, body=%wide.region_15.17_spmd.sunk | while | flops 511146496 | bytes 26125436 | solution.py:215
  1526.3 6.3 fusion.88
  1532.7 6.5 fusion.87
  1539.1 12.8 add_convert_fusion
  1552.0 11.7 fusion.67
  1563.8 10.1 fusion.89
  1573.9 4.7 convolution_bitcast_fusion.2
  1579.9 4.7 convolution_bitcast_fusion
  1587.3 4.7 convolution_bitcast_fusion.1
  1595.2 24.4 %all-reduce.3 = (f32[2,3,64]{2,1,0:T(4,128)S(1)}, f32[12,64]{1,0:T(8,128)S(1)}) all-reduce(f32[2,3,64]{2,1,0:T(4,128)S(1)} %pad_maximum_fusion.1, f32[12,64]{1,0:T(8,128)S(1)} %reshape.274), channel_id=12, replica_groups=mesh['dp'=8,'tensor'=4] {'dp'}, use_global_device_ids=true, to_apply=%region_27.28.clone | all-reduce | flops 1152 | bytes 9216
  1622.7 38.4 %reduce-scatter.28.cloned.1.call-done = bf16[1024,768]{1,0:T(8,128)(2,1)} async-done(((bf16[4096,768]{1,0:T(8,128)(2,1)}), bf16[1024,768]{1,0:T(8,128)(2,1)}) %reduce-scatter.28.cloned.1.call-update) | async-done | bytes 1572880 | tf_op jit(solution)/shard_map/reduce_scatter | solution.py:229
  1661.1 5.4 convert_reduce_fusion.3
  1666.5 41.1 %all-reduce.2 = f32[6,768]{1,0:T(8,128)S(1)} all-reduce(f32[6,768]{1,0:T(8,128)S(1)} %stack.59), channel_id=14, replica_groups=mesh['dp'=8,'tensor'=4] {'dp','tensor'}, use_global_device_ids=true, to_apply=%region_36.37.clone | all-reduce | flops 4608 | bytes 36864
  1708.5 46.1 %reduce-scatter.32.cloned.1.call-done = f32[768,96]{0,1:T(8,128)} async-done(((f32[768,768]{0,1:T(8,128)}), f32[768,96]{0,1:T(8,128)}) %reduce-scatter.32.cloned.1.call-update) | async-done | bytes 294928 | tf_op jit(solution)/shard_map/reduce_scatter | solution.py:241
  1754.7 38.5 %reduce-scatter.34.cloned.1.call-done = f32[96,192]{1,0:T(8,128)} async-done(((f32[768,192]{1,0:T(8,128)}), f32[96,192]{1,0:T(8,128)}) %reduce-scatter.34.cloned.1.call-update) | async-done | bytes 73744
  1793.2 38.7 %reduce-scatter.38.cloned.1.call-done = f32[96,192]{1,0:T(8,128)} async-done(((f32[768,192]{1,0:T(8,128)}), f32[96,192]{1,0:T(8,128)}) %reduce-scatter.38.cloned.1.call-update) | async-done | bytes 73744
  1831.9 38.6 %reduce-scatter.36.cloned.1.call-done = f32[96,192]{1,0:T(8,128)} async-done(((f32[768,192]{1,0:T(8,128)}), f32[96,192]{1,0:T(8,128)}) %reduce-scatter.36.cloned.1.call-update) | async-done | bytes 73744
  (282 shorter events, 203.3 us)
Async XLA Ops:
  7.2 553.2 %copy-start = (bf16[768,768]{1,0:T(8,128)(2,1)S(1)}, bf16[768,768]{1,0:T(8,128)(2,1)}, u32[]{:S(2)}) copy-start(bf16[768,768]{1,0:T(8,128)(2,1)} %param.33) | copy-start | bytes 3538948
  7.2 298.6 %reduce-scatter.22.cloned.1.call-start = ((), (), s32[]{:S(2)}) async-start(), calls=%async_computation.10 | async-start | bytes 15728640 | tf_op jit(solution)/shard_map/reduce_scatter | solution.py:145
  8.6 7.3 copy-start.19
  13.7 3.4 copy-start.15
  19.2 1.2 copy-start.17
  79.9 3.5 copy-start.10
  79.9 4.7 copy-start.14
  83.4 1.1 copy-start.6
  91.0 0.7 copy-start.25
  91.0 705.2 %reduce-scatter.24.cloned.1.call-start = ((), (), s32[]{:S(2)}) async-start(), calls=%async_computation.11 | async-start | bytes 15728640 | tf_op jit(solution)/shard_map/reduce_scatter | solution.py:181
  91.7 358.3 %copy-start.26 = (bf16[768]{0:T(1024)(128)(2,1)S(1)}, bf16[768]{0:T(1024)(128)(2,1)}, u32[]{:S(2)}) copy-start(bf16[768]{0:T(1024)(128)(2,1)} %param.31) | copy-start | bytes 4612
  91.7 358.3 %copy-start.27 = (bf16[768]{0:T(1024)(128)(2,1)S(1)}, bf16[768]{0:T(1024)(128)(2,1)}, u32[]{:S(2)}) copy-start(bf16[768]{0:T(1024)(128)(2,1)} %param.34) | copy-start | bytes 4612
  91.7 358.3 %copy-start.28 = (bf16[768]{0:T(1024)(128)(2,1)S(1)}, bf16[768]{0:T(1024)(128)(2,1)}, u32[]{:S(2)}) copy-start(bf16[768]{0:T(1024)(128)(2,1)} %param.32) | copy-start | bytes 4612
  310.1 73.1 %collective-permute-start = (f32[1024,768]{1,0:T(8,128)}, f32[1024,768]{1,0:T(8,128)}, u32[]{:S(2)}, u32[]{:S(2)}) collective-permute-start(f32[1024,768]{1,0:T(8,128)} %add_add_fusion.1), channel_id=1, source_target_pairs={{0,1},{1,2},{2,3},{3,0},{4,5},{5,6},{6,7},{7,4},{8,9},{9,10},{10,1... | collective-permute-start | bytes 9437192 | tf_op jit(solution)/shard_map/ppermute | solution.py:163
  311.6 139.0 %collective-permute-start.2 = (f32[1024,768]{1,0:T(8,128)}, f32[1024,768]{1,0:T(8,128)}, u32[]{:S(2)}, u32[]{:S(2)}) collective-permute-start(f32[1024,768]{1,0:T(8,128)} %add_add_fusion.1), channel_id=1, source_target_pairs={{1,0},{2,1},{3,2},{0,3},{5,4},{6,5},{7,6},{4,7},{9,8},{10,9},{11,1... | collective-permute-start | bytes 9437192 | tf_op jit(solution)/shard_map/ppermute | solution.py:166
  383.3 133.6 %collective-permute-start.1 = (f32[1024,768]{1,0:T(8,128)}, f32[1024,768]{1,0:T(8,128)}, u32[]{:S(2)}, u32[]{:S(2)}) collective-permute-start(f32[1024,768]{1,0:T(8,128)} %collective-permute-done), channel_id=1, source_target_pairs={{0,1},{1,2},{2,3},{3,0},{4,5},{5,6},{6,7},{7,4},{8,9},{9,10},{10,1... | collective-permute-start | bytes 9437192 | tf_op jit(solution)/shard_map/ppermute | solution.py:163
  543.0 8.2 copy-start.3
  560.4 16.4 copy-start.32
  574.2 2.6 copy-start.34
  584.9 0.7 copy-start.30
  584.9 338.6 %all-gather.3.cloned.1.call-start = ((), (), s32[]{:S(2)}) async-start(), calls=%async_computation.12 | async-start | bytes 7864320 | tf_op jit(solution)/shard_map/all_gather | solution.py:194
  799.5 4.9 copy-start.4
  799.5 2.5 copy-start.8
  807.0 351.4 %reduce-scatter.26.cloned.1.call-start = ((), (), s32[]{:S(2)}) async-start(), calls=%async_computation.13 | async-start | bytes 15728640 | tf_op jit(solution)/shard_map/reduce_scatter | solution.py:201
  937.3 2.6 copy-start.5
  948.2 435.6 %all-gather.5.cloned.1.call-start = ((), (), s32[]{:S(2)}) async-start(), calls=%async_computation.14 | async-start | bytes 15728640 | tf_op jit(solution)/shard_map/all_gather | solution.py:204
  1164.4 456.5 %reduce-scatter.40.cloned.1.call-start = ((), (), s32[]{:S(2)}) async-start(), calls=%async_computation.21 | async-start | bytes 884736
  1393.5 14.3 copy-start.7
  1403.3 4.5 copy-start.2
  1418.1 242.9 %reduce-scatter.28.cloned.1.call-start = ((), (), s32[]{:S(2)}) async-start(), calls=%async_computation.15 | async-start | bytes 7864320 | tf_op jit(solution)/shard_map/reduce_scatter | solution.py:229
  1522.8 3.5 copy-start.11
  1522.8 2.0 copy-start.9
  1524.3 14.8 copy-start.13
  1524.8 1.6 copy-start.18
  1526.3 6.4 copy-start.12
  1526.3 6.3 copy-start.20
  1532.7 6.5 copy-start.16
  1551.9 156.6 %reduce-scatter.30.cloned.1.call-start = ((), (), s32[]{:S(2)}) async-start(), calls=%async_computation.16 | async-start | bytes 2654208 | tf_op jit(solution)/shard_map/reduce_scatter | solution.py:240
  1563.7 191.0 %reduce-scatter.32.cloned.1.call-start = ((), (), s32[]{:S(2)}) async-start(), calls=%async_computation.17 | async-start | bytes 2654208 | tf_op jit(solution)/shard_map/reduce_scatter | solution.py:241
  1573.9 219.3 %reduce-scatter.34.cloned.1.call-start = ((), (), s32[]{:S(2)}) async-start(), calls=%async_computation.18 | async-start | bytes 884736
  1579.8 6.1 copy-start.33
  1579.8 7.3 copy-start.23
  1579.8 7.3 copy-start.22
  1579.9 7.3 copy-start.21
  1579.9 7.3 copy-start.24
  1579.9 252.0 %reduce-scatter.38.cloned.1.call-start = ((), (), s32[]{:S(2)}) async-start(), calls=%async_computation.20 | async-start | bytes 884736
  1585.8 284.7 %reduce-scatter.36.cloned.1.call-start = ((), (), s32[]{:S(2)}) async-start(), calls=%async_computation.19 | async-start | bytes 884736
  1620.9 249.5 %copy-start.1 = (bf16[768,768]{1,0:T(8,128)(2,1)S(1)}, bf16[768,768]{1,0:T(8,128)(2,1)}, u32[]{:S(2)}) copy-start(bf16[768,768]{1,0:T(8,128)(2,1)} %param.33) | copy-start | bytes 3538948
  (2 other events, 1.4 us)
Sparse Core Ops, SparseCore 0:
  91.1 214.6 reduce-scatter.21
  585.1 211.0 reduce-scatter.23
  807.1 116.3 all-gather.2
  948.3 210.0 reduce-scatter.25
  1164.6 219.1 all-gather.4
  1418.2 33.0 reduce-scatter.39
  1552.0 108.9 reduce-scatter.27
  1665.0 43.5 reduce-scatter.29
  1712.5 42.1 reduce-scatter.31
  1758.2 34.9 reduce-scatter.33
  1796.9 34.9 reduce-scatter.37
  1835.5 34.9 reduce-scatter.35
